TPU v7x, 256 devices: a whole 4x4x8 slice. The times are simulated.
256 devices in a mesh: dp: 16 (over x, y), shard: 16 (over z, core).
Axes of the slice: x: 4, y: 4, z: 8, core: 2. Of those that a mesh axis runs over, the one named last changes fastest.
Arguments:
- gradient: bfloat16 [16, 4096, 6144], P('dp', None, 'shard'), may hold values from -400 to 400
- error_buffer: bfloat16 [16, 4096, 6144], P('dp', None, 'shard'), may hold values from -6 to 6
- right_init: float32 [6144, 32], P('shard'), may hold values from -6 to 6
- first_moment: float32 [4096, 6144], P(('dp', 'shard')), may hold values from -0.06 to 0.06
- second_moment: float32 [4096, 6144], P(('dp', 'shard')), may hold values from 0.001 to 0.01
Outputs:
- error_out: bfloat16 [16, 4096, 6144], P('dp', None, 'shard')
- first_out: float32 [4096, 6144], P(('dp', 'shard'))
- second_out: float32 [4096, 6144], P(('dp', 'shard'))
- direction: float32 [4096, 6144], P(('dp', 'shard'))
All inputs are finite; a program needn't handle non-finite values.
Results may differ from a plain program's by a relative error of at most 0.009.
Values sent between devices are 32-bit elements; how exact they have to be, the bound alone decides.
A program may use at most 64 MiB of HBM per device.

v0:
```python
import jax
import jax.numpy as jnp
from jax import lax
from jax.sharding import PartitionSpec as P

D = 4096
F = 6144
R = 32
CLIP_LEVEL = 0.9
BETA_ONE = 0.9
BETA_TWO = 0.95
EPSILON = 1e-08


def cut_along(x, dim, count):
    shape = x.shape
    tiles = x.reshape(*shape[:dim], count, shape[dim] // count, *shape[dim + 1 :])
    return jnp.moveaxis(tiles, dim, 0)


def sent_and_summed(x, axis, dim):
    tiles = cut_along(x, dim, lax.axis_size(axis))
    arrived = lax.all_to_all(tiles, axis, split_axis=0, concat_axis=0, tiled=True)
    return arrived.sum(axis=0)


def sent_to_all(x, axis):
    count = lax.axis_size(axis)
    return lax.all_to_all(jnp.broadcast_to(x[None], (count, *x.shape)), axis, 0, 0, tiled=True)


def taken_together(x, axis):
    return sent_to_all(x, axis).sum(axis=0)


def laid_out(tiles, dim):
    shape = list(tiles.shape[1:])
    shape[dim] *= tiles.shape[0]
    return jnp.moveaxis(tiles, 0, dim).reshape(shape)


def collect(x, axis, dim):
    return laid_out(sent_to_all(x, axis), dim)


def orthonormal(left_raw, gram_matrix):
    width = gram_matrix.shape[0]
    ridge_shift = 1e-06 * jnp.trace(gram_matrix) / width
    lower_factor = jnp.linalg.cholesky(
        gram_matrix + ridge_shift * jnp.eye(width, dtype=jnp.float32)
    )
    return lax.linalg.triangular_solve(
        lower_factor, left_raw, left_side=False, lower=True, transpose_a=True
    )


def local(gradient, error_buffer, right_init, first_moment, second_moment):
    replica_count = lax.axis_size("dp")
    shard_count = lax.axis_size("shard")
    merged = (gradient[0].astype(jnp.float32) + error_buffer[0].astype(jnp.float32)).astype(
        jnp.bfloat16
    )
    total_rows = merged.shape[0]
    left_part = jnp.dot(merged, right_init.astype(jnp.bfloat16), preferred_element_type=jnp.float32)
    row_share = sent_and_summed(left_part, "shard", 0)
    row_share = taken_together(row_share, "dp") / replica_count
    left_raw = lax.all_gather(row_share, "shard", axis=0, tiled=True)
    gram_matrix = jnp.dot(left_raw.T, left_raw, precision=lax.Precision.HIGHEST)
    left_orth = orthonormal(left_raw, gram_matrix)
    right_part = lax.dot_general(
        merged,
        left_orth.astype(jnp.bfloat16),
        (((0,), (0,)), ((), ())),
        preferred_element_type=jnp.float32,
    )
    right_mean = taken_together(right_part, "dp") / replica_count
    update = jnp.dot(left_orth, right_mean.T, precision=lax.Precision.HIGHEST)
    error_out = (merged.astype(jnp.float32) - update).astype(jnp.bfloat16)[None]
    slab_size = total_rows // replica_count
    own_count = slab_size // shard_count
    right_full = collect(right_mean, "shard", 0)
    first_row = (lax.axis_index("dp") * shard_count + lax.axis_index("shard")) * own_count
    left_own = lax.dynamic_slice_in_dim(left_orth, first_row, own_count, 0)
    owned_rows = jnp.dot(left_own, right_full.T, precision=lax.Precision.HIGHEST)
    square_total = jnp.sum(right_full * right_full)
    grad_norm = jnp.sqrt(square_total)
    clip_level = CLIP_LEVEL * jnp.sqrt(jnp.float32(R * (D + F)))
    scaled = owned_rows * (clip_level / jnp.maximum(grad_norm, clip_level))
    first_out = BETA_ONE * first_moment + (1.0 - BETA_ONE) * scaled
    second_out = BETA_TWO * second_moment + (1.0 - BETA_TWO) * scaled * scaled
    direction = first_out / (jnp.sqrt(second_out) + EPSILON)
    return (error_out, first_out, second_out, direction)


def solution(mesh):
    return jax.shard_map(
        local,
        mesh=mesh,
        in_specs=(
            P("dp", None, "shard"),
            P("dp", None, "shard"),
            P("shard", None),
            P(("dp", "shard"), None),
            P(("dp", "shard"), None),
        ),
        out_specs=(
            P("dp", None, "shard"),
            P(("dp", "shard"), None),
            P(("dp", "shard"), None),
            P(("dp", "shard"), None),
        ),
        check_vma=False,
    )
```

profile of v0, /device:TPU:1, one launch (start us, length us, event | category | flops | bytes accessed | tf_op | source)
XLA Modules:
  0.0 137.0 jit_solution(12787354762281012879)
XLA Ops:
  0.6 3.7 %add_convert_fusion = bf16[1,4096,384]{2,1,0:T(8,128)(2,1)S(1)} fusion(bf16[1,4096,384]{2,1,0:T(8,128)(2,1)} %param.6, bf16[1,4096,384]{2,1,0:T(8,128)(2,1)} %param.5), kind=kLoop, calls=%fused_computation.2 | loop fusion | flops 6291456 | bytes 9437184 | tf_op jit(solution)/shard_map/convert_element_type | solution.py:60
  4.3 1.1 fusion.5
  5.4 27.2 %all_to_all.20 = f32[16,256,32]{1,2,0:T(8,128)} all-to-all(f32[16,256,32]{1,2,0:T(8,128)S(1)} %fusion.5), channel_id=1, replica_groups=mesh['dp'=16,'shard'=16] {'shard'}, dimensions={0} | all-to-all | bytes 1048576 | tf_op jit(solution)/shard_map/all_to_all | solution.py:23
  32.6 1.1 reduce_sum.46
  33.7 18.0 %all_to_all.21 = f32[16,256,32]{1,2,0:T(8,128)} all-to-all(f32[16,256,32]{1,2,0:T(8,128)S(1)} %broadcast_in_dim.14), channel_id=1, replica_groups=mesh['dp'=16,'shard'=16] {'dp'}, dimensions={0} | all-to-all | bytes 1048576 | tf_op jit(solution)/shard_map/all_to_all | solution.py:29
  51.7 1.1 reduce_sum.47
  52.8 15.9 %all_gather.3 = f32[4096,32]{0,1:T(8,128)S(1)} all-gather(f32[256,32]{0,1:T(8,128)S(1)} %broadcast_multiply_fusion.1), channel_id=1, replica_groups=mesh['dp'=16,'shard'=16] {'shard'}, dimensions={0}, use_global_device_ids=true | all-gather | bytes 557056 | tf_op jit(solution)/shard_map/all_gather | solution.py:67
  68.7 0.8 copy-done
  69.5 1.2 select_reduce_fusion.1
  71.4 2.9 %cholesky.17 = f32[32,32]{1,0:T(8,128)S(1)} custom-call(f32[32,32]{1,0:T(8,128)S(1)} %fusion.12), custom_call_target="Cholesky" | custom-call | tf_op jit(solution)/shard_map/jit(cholesky)/cholesky | solution.py:49
  74.3 0.6 compare_reduce_fusion
  75.0 0.7 fusion.8
  75.6 2.4 %custom-call.6 = f32[1,32,32]{1,2,0:T(8,128)S(1)} custom-call(f32[1,32,32]{2,1,0:T(8,128)S(1)} %fusion.8), custom_call_target="InvertDiagBlocksLowerTriangular" | custom-call | tf_op jit(solution)/shard_map/triangular_solve | solution.py:52
  78.0 1.7 %fusion.9 = f32[4096,32]{0,1:T(8,128)S(1)} fusion(f32[4096,32]{0,1:T(8,128)} %copy-done, f32[1,32,32]{1,2,0:T(8,128)S(1)} %custom-call.6), kind=kOutput, calls=%fused_computation.18 | convolution fusion | flops 50331648 | bytes 1052672 | tf_op jit(solution)/shard_map/triangular_solve | solution.py:52
  79.7 0.8 copy-done.1
  81.2 16.7 %all_to_all.22 = f32[16,384,32]{1,2,0:T(8,128)} all-to-all(f32[16,384,32]{1,2,0:T(8,128)S(1)} %broadcast_in_dim.16), channel_id=1, replica_groups=mesh['dp'=16,'shard'=16] {'dp'}, dimensions={0} | all-to-all | bytes 1572864 | tf_op jit(solution)/shard_map/all_to_all | solution.py:29
  97.9 1.2 reduce_sum.49
  99.1 1.0 broadcast_in_dim.31
  100.1 7.3 %all-to-all-start.3 = ((f32[16,384,32]{1,2,0:T(8,128)}), f32[16,384,32]{1,2,0:T(8,128)}, u32[]{:S(2)}, u32[]{:S(2)}) async-start(f32[16,384,32]{1,2,0:T(8,128)} %broadcast_in_dim.31), calls=%async_computation.3 | async-start | bytes 1572864 | tf_op jit(solution)/shard_map/all_to_all | solution.py:29
  107.4 7.8 %fusion = bf16[1,4096,384]{2,1,0:T(8,128)(2,1)} fusion(f32[4096,32]{0,1:T(8,128)} %copy-done.1, bf16[1,4096,384]{2,1,0:T(8,128)(2,1)S(1)} %add_convert_fusion, f32[384,32]{0,1:T(8,128)S(1)} %reduce_sum.49), kind=kOutput, calls=%fused_computation.3 | convolution fusion | flops 608710656 | bytes 6864896 | tf_op jit(solution)/shard_map/dot_general | solution.py:77
  115.2 15.0 %all-to-all-done.3 = f32[16,384,32]{1,2,0:T(8,128)} async-done(((f32[16,384,32]{1,2,0:T(8,128)}), f32[16,384,32]{1,2,0:T(8,128)}, u32[]{:S(2)}, u32[]{:S(2)}) %all-to-all-start.3) | async-done | bytes 786464 | tf_op jit(solution)/shard_map/all_to_all | solution.py:29
  130.2 1.9 %multiply_reduce_fusion = f32[]{:T(128)} fusion(f32[16,384,32]{1,2,0:T(8,128)} %all-to-all-done.3), kind=kLoop, calls=%fused_computation.6 | loop fusion | flops 393215 | bytes 786436 | tf_op jit(solution)/shard_map/reduce_sum | solution.py:85
  132.9 1.2 copy.16
  134.1 3.0 %add_divide_fusion = (f32[16,6144]{1,0:T(8,128)}, f32[16,6144]{1,0:T(8,128)}, f32[16,6144]{1,0:T(8,128)}) fusion(f32[16,6144]{1,0:T(8,128)} %param.9, f32[16,6144]{1,0:T(8,128)} %param.8, f32[]{:T(128)S(6)} %div.36, f32[6144,32]{0,1:T(8,128)S(1)} %bitcast.30, f32[4096,32]{0,1:T(8,128)} %copy-done.1, s32[]{:T(128)S(6)} %select_n.14), kind=kOutput, calls=%fused_computation.9 | convolution fusion | flops 38731776 | bytes 2768904 | tf_op jit(solution)/shard_map/dot_general | solution.py:84
  (12 shorter events, 0.8 us)
Async XLA Ops:
  0.6 3.7 %copy-start.2 = (f32[384,32]{0,1:T(8,128)S(1)}, f32[384,32]{0,1:T(8,128)}, u32[]{:S(2)}) copy-start(f32[384,32]{0,1:T(8,128)} %param.7) | copy-start | bytes 147460
  68.7 0.8 copy-start
  79.7 0.8 copy-start.1
  100.1 30.1 %all-to-all-start.3 = ((f32[16,384,32]{1,2,0:T(8,128)}), f32[16,384,32]{1,2,0:T(8,128)}, u32[]{:S(2)}, u32[]{:S(2)}) async-start(f32[16,384,32]{1,2,0:T(8,128)} %broadcast_in_dim.31), calls=%async_computation.3 | async-start | bytes 1572864 | tf_op jit(solution)/shard_map/all_to_all | solution.py:29
where the time goes:
time: 138 us; the launch traced here: 137 us
  blocking collectives  77.8 us (56%)
  other arithmetic  15.6 us (11%)
  matrix products  15.2 us (11%)
  waiting for transfers between devices  15 us (11%)
  starting transfers between devices  7.33 us (5%)
  local copies, waits for them, and re-layouts  3.97 us (3%)
  between operations  2.13 us (2%)
    all_to_all x2, blocking collectives, sent_to_all(): lax.all_to_all(jnp.broadcast_to(x[None], (count, *x.shape)), axis, 0, 0,...  34.7 us
    all_to_all x1, blocking collectives, sent_and_summed(): lax.all_to_all(tiles, axis, split_axis=0, concat_axis=0, tiled=True)  27.2 us
    all_gather x1, blocking collectives, local(): left_raw = lax.all_gather(row_share, 'shard', axis=0, tiled=True)  15.9 us
    all_to_all x1, waiting for transfers between devices, sent_to_all(): lax.all_to_all(jnp.broadcast_to(x[None], (count, *x.shape)), axis, 0, 0,...  15 us
    dot_general x1, matrix products, local(): update = jnp.dot(left_orth, right_mean.T, precision=lax.Precision.HIGHEST)  7.79 us
    all_to_all x1, starting transfers between devices, sent_to_all(): lax.all_to_all(jnp.broadcast_to(x[None], (count, *x.shape)), axis, 0, 0,...  7.33 us
    convert_element_type x1, other arithmetic, local(): (gradient[0].astype(jnp.float32) + error_buffer[0].astype(jnp.float32)).a...  3.66 us
    another operation x3, other arithmetic, orthonormal(): jnp.linalg.cholesky(gram_matrix + ridge_shift * jnp.eye(width, dtype=jnp....  3.59 us
  transfers between devices with their start and end apart: 1, of which 1 were waited for; matrix products, arithmetic and copies ran while one was open for 6% of the time, Pallas kernels for 0%

commit v1 on v0

--- a/solution.py
+++ b/solution.py
@@ -64,7 +64,15 @@
     left_part = jnp.dot(merged, right_init.astype(jnp.bfloat16), preferred_element_type=jnp.float32)
     row_share = sent_and_summed(left_part, "shard", 0)
     row_share = taken_together(row_share, "dp") / replica_count
-    left_raw = lax.all_gather(row_share, "shard", axis=0, tiled=True)
+    left_raw = jnp.concatenate(
+        lax.all_to_all(
+            jnp.stack(tuple((row_share for _ in range(lax.axis_size("shard")))), axis=0),
+            axis_name="shard",
+            split_axis=0,
+            concat_axis=0,
+        ),
+        axis=0,
+    )
     gram_matrix = jnp.dot(left_raw.T, left_raw, precision=lax.Precision.HIGHEST)
     left_orth = orthonormal(left_raw, gram_matrix)
     right_part = lax.dot_general(

time: 138 us -> 139 us (level)
  blocking collectives: 77.8 us -> 82.9 us
  starting transfers between devices: 7.33 us -> 4.18 us
    all_to_all x0 -> x1, blocking collectives: none -> 20.8 us  [local(): lax.all_to_all(jnp.stack(tuple((row_share for _ in range(lax.axis_size('s...]
    all_gather x1 -> x0, blocking collectives: 15.9 us -> none  [local(): left_raw = lax.all_gather(row_share, 'shard', axis=0, tiled=True)]
    all_to_all x1, starting transfers between devices: 7.33 us -> 4.18 us  [sent_to_all(): lax.all_to_all(jnp.broadcast_to(x[None], (count, *x.shape)), axis, 0, 0,...]
where the time goes in v1:
time: 139 us
  blocking collectives  82.9 us (60%)
  other arithmetic  15.6 us (11%)
  waiting for transfers between devices  14.6 us (11%)
  matrix products  14.1 us (10%)
  local copies, waits for them, and re-layouts  5.11 us (4%)
  starting transfers between devices  4.18 us (3%)
  between operations  2.16 us (2%)
    all_to_all x2, blocking collectives, sent_to_all(): lax.all_to_all(jnp.broadcast_to(x[None], (count, *x.shape)), axis, 0, 0,...  35 us
    all_to_all x1, blocking collectives, sent_and_summed(): lax.all_to_all(tiles, axis, split_axis=0, concat_axis=0, tiled=True)  27.2 us
    all_to_all x1, blocking collectives, local(): lax.all_to_all(jnp.stack(tuple((row_share for _ in range(lax.axis_size('s...  20.8 us
    all_to_all x1, waiting for transfers between devices, sent_to_all(): lax.all_to_all(jnp.broadcast_to(x[None], (count, *x.shape)), axis, 0, 0,...  14.6 us
    dot_general x1, matrix products, local(): update = jnp.dot(left_orth, right_mean.T, precision=lax.Precision.HIGHEST)  7.8 us
    all_to_all x1, starting transfers between devices, sent_to_all(): lax.all_to_all(jnp.broadcast_to(x[None], (count, *x.shape)), axis, 0, 0,...  4.18 us
    convert_element_type x1, other arithmetic, local(): (gradient[0].astype(jnp.float32) + error_buffer[0].astype(jnp.float32)).a...  3.66 us
    another operation x3, other arithmetic, orthonormal(): jnp.linalg.cholesky(gram_matrix + ridge_shift * jnp.eye(width, dtype=jnp....  3.59 us
  transfers between devices with their start and end apart: 1, of which 1 were waited for; matrix products, arithmetic and copies ran while one was open for 6% of the time, Pallas kernels for 0%

profile of v1, /device:TPU:1, one launch (start us, length us, event | category | flops | bytes accessed | tf_op | source)
XLA Modules:
  0.0 138.8 jit_solution(14257257940599692220)
XLA Ops:
  0.6 3.7 %add_convert_fusion = bf16[1,4096,384]{2,1,0:T(8,128)(2,1)S(1)} fusion(bf16[1,4096,384]{2,1,0:T(8,128)(2,1)} %param.6, bf16[1,4096,384]{2,1,0:T(8,128)(2,1)} %param.5), kind=kLoop, calls=%fused_computation.2 | loop fusion | flops 6291456 | bytes 9437184 | tf_op jit(solution)/shard_map/convert_element_type | solution.py:60
  4.3 1.1 fusion.5
  5.4 27.2 %all_to_all.25 = f32[16,256,32]{1,2,0:T(8,128)} all-to-all(f32[16,256,32]{1,2,0:T(8,128)S(1)} %fusion.5), channel_id=1, replica_groups=mesh['dp'=16,'shard'=16] {'shard'}, dimensions={0} | all-to-all | bytes 1048576 | tf_op jit(solution)/shard_map/all_to_all | solution.py:23
  32.6 1.1 reduce_sum.46
  33.7 18.0 %all_to_all.26 = f32[16,256,32]{1,2,0:T(8,128)} all-to-all(f32[16,256,32]{1,2,0:T(8,128)S(1)} %broadcast_in_dim.14), channel_id=1, replica_groups=mesh['dp'=16,'shard'=16] {'dp'}, dimensions={0} | all-to-all | bytes 1048576 | tf_op jit(solution)/shard_map/all_to_all | solution.py:29
  51.7 1.1 reduce_sum.47
  52.8 20.8 %all_to_all.27 = f32[16,256,32]{1,2,0:T(8,128)S(1)} all-to-all(f32[16,256,32]{1,2,0:T(8,128)S(1)} %stack.2), channel_id=1, replica_groups=mesh['dp'=16,'shard'=16] {'shard'}, dimensions={0} | all-to-all | bytes 1048576 | tf_op jit(solution)/shard_map/all_to_all | solution.py:68
  73.6 0.8 copy-done
  74.4 1.2 select_reduce_fusion.1
  76.3 2.9 %cholesky.17 = f32[32,32]{1,0:T(8,128)S(1)} custom-call(f32[32,32]{1,0:T(8,128)S(1)} %fusion.12), custom_call_target="Cholesky" | custom-call | tf_op jit(solution)/shard_map/jit(cholesky)/cholesky | solution.py:49
  79.2 0.6 compare_reduce_fusion
  79.9 0.7 fusion.8
  80.5 2.4 %custom-call.6 = f32[1,32,32]{1,2,0:T(8,128)S(1)} custom-call(f32[1,32,32]{2,1,0:T(8,128)S(1)} %fusion.8), custom_call_target="InvertDiagBlocksLowerTriangular" | custom-call | tf_op jit(solution)/shard_map/triangular_solve | solution.py:52
  83.0 1.1 copy.19
  84.7 0.8 copy-done.1
  86.1 17.0 %all_to_all.28 = f32[16,384,32]{1,2,0:T(8,128)} all-to-all(f32[16,384,32]{1,2,0:T(8,128)S(1)} %broadcast_in_dim.16), channel_id=1, replica_groups=mesh['dp'=16,'shard'=16] {'dp'}, dimensions={0} | all-to-all | bytes 1572864 | tf_op jit(solution)/shard_map/all_to_all | solution.py:29
  103.1 1.2 reduce_sum.49
  104.3 1.0 broadcast_in_dim.31
  105.3 4.2 %all-to-all-start.4 = ((f32[16,384,32]{1,2,0:T(8,128)}), f32[16,384,32]{1,2,0:T(8,128)}, u32[]{:S(2)}, u32[]{:S(2)}) async-start(f32[16,384,32]{1,2,0:T(8,128)} %broadcast_in_dim.31), calls=%async_computation.4 | async-start | bytes 1572864 | tf_op jit(solution)/shard_map/all_to_all | solution.py:29
  109.5 7.8 %fusion = bf16[1,4096,384]{2,1,0:T(8,128)(2,1)} fusion(f32[4096,32]{0,1:T(8,128)} %copy-done.1, bf16[1,4096,384]{2,1,0:T(8,128)(2,1)S(1)} %add_convert_fusion, f32[384,32]{0,1:T(8,128)S(1)} %reduce_sum.49), kind=kOutput, calls=%fused_computation.3 | convolution fusion | flops 608710656 | bytes 6864896 | tf_op jit(solution)/shard_map/dot_general | solution.py:85
  117.3 14.6 %all-to-all-done.4 = f32[16,384,32]{1,2,0:T(8,128)} async-done(((f32[16,384,32]{1,2,0:T(8,128)}), f32[16,384,32]{1,2,0:T(8,128)}, u32[]{:S(2)}, u32[]{:S(2)}) %all-to-all-start.4) | async-done | bytes 786464 | tf_op jit(solution)/shard_map/all_to_all | solution.py:29
  132.0 1.9 %multiply_reduce_fusion = f32[]{:T(128)} fusion(f32[16,384,32]{1,2,0:T(8,128)} %all-to-all-done.4), kind=kLoop, calls=%fused_computation.7 | loop fusion | flops 393215 | bytes 786436 | tf_op jit(solution)/shard_map/reduce_sum | solution.py:93
  134.6 1.2 copy.20
  135.8 3.0 %add_divide_fusion = (f32[16,6144]{1,0:T(8,128)}, f32[16,6144]{1,0:T(8,128)}, f32[16,6144]{1,0:T(8,128)}) fusion(f32[16,6144]{1,0:T(8,128)} %param.9, f32[16,6144]{1,0:T(8,128)} %param.8, f32[]{:T(128)S(6)} %div.36, f32[6144,32]{0,1:T(8,128)S(1)} %bitcast.35, f32[4096,32]{0,1:T(8,128)} %copy-done.1, s32[]{:T(128)S(6)} %select_n.14), kind=kOutput, calls=%fused_computation.10 | convolution fusion | flops 38731776 | bytes 2768904 | tf_op jit(solution)/shard_map/dot_general | solution.py:92
  (14 shorter events, 1.5 us)
Async XLA Ops:
  0.6 3.7 %copy-start.2 = (f32[384,32]{0,1:T(8,128)S(1)}, f32[384,32]{0,1:T(8,128)}, u32[]{:S(2)}) copy-start(f32[384,32]{0,1:T(8,128)} %param.7) | copy-start | bytes 147460
  73.6 0.8 copy-start
  84.7 0.8 copy-start.1
  105.3 26.6 %all-to-all-start.4 = ((f32[16,384,32]{1,2,0:T(8,128)}), f32[16,384,32]{1,2,0:T(8,128)}, u32[]{:S(2)}, u32[]{:S(2)}) async-start(f32[16,384,32]{1,2,0:T(8,128)} %broadcast_in_dim.31), calls=%async_computation.4 | async-start | bytes 1572864 | tf_op jit(solution)/shard_map/all_to_all | solution.py:29
